TPU v7x, 512 devices: a whole 4x4x16 slice. The times are simulated.
512 devices in a mesh: seq: 64 (over z, y), tp: 8 (over x, core).
Axes of the slice: x: 4, y: 4, z: 16, core: 2. Of those that a mesh axis runs over, the one named last changes fastest.
Arguments:
- query_proj: bfloat16 [4096, 8192], P('tp', 'seq'), may hold values from -6 to 6
- key_proj: bfloat16 [4096, 8192], P('tp', 'seq'), may hold values from -6 to 6
- value_proj: bfloat16 [4096, 8192], P('tp', 'seq'), may hold values from -6 to 6
- short_taps: float32 [3, 3, 4096], P(None, None, 'tp'), may hold values from -3.5 to 3.5
- long_filters: float32 [4096, 8192], P(('tp', 'seq')), may hold values from -2 to 2
- out_weight: bfloat16 [4096, 8192], P('seq', 'tp'), may hold values from -0.09375 to 0.09375
Outputs:
- block_out: bfloat16 [8192, 8192], P('seq', 'tp')
All inputs are finite; a program needn't handle non-finite values.
Results may differ from a plain program's by a relative error of at most 0.0058.
Values may be sent and summed in bfloat16 or wider, within the bound.
A program may use at most 64 MiB of HBM per device.

v0:
```python
import math
import jax
import jax.numpy as jnp
from jax import lax
from jax.sharding import PartitionSpec as P

precise = lax.Precision.HIGHEST


def shifted(value, axis, steps):
    count = lax.axis_size(axis)
    initial, last = (max(0, -steps), min(count, count - steps))
    return lax.ppermute(value, axis, [(source, source + steps) for source in range(initial, last)])


def short_filter(extended, tap_weights):
    return (
        tap_weights[0][:, None] * extended[:, 2:]
        + tap_weights[1][:, None] * extended[:, 1:-1]
        + tap_weights[2][:, None] * extended[:, :-2]
    )


def phase_table(period, out_size, in_size, direction):
    out_index = lax.broadcasted_iota(jnp.int32, (out_size, in_size), 0)
    in_index = lax.broadcasted_iota(jnp.int32, (out_size, in_size), 1)
    phase_angle = (out_index * in_index % period).astype(jnp.float32) * (
        direction * 2.0 * math.pi / period
    )
    return (jnp.cos(phase_angle), jnp.sin(phase_angle))


def left_apply(phase, signal):
    return jnp.einsum("kn,cnm->ckm", phase, signal, precision=precise)


def right_apply(signal, phase):
    return jnp.einsum("ckn,nm->ckm", signal, phase, precision=precise)


def forward_spectrum(signal, inner_size):
    channels_here, length = signal.shape
    period = 2 * length
    outer_size = period // inner_size
    blocks = signal.reshape(channels_here, outer_size // 2, inner_size)
    left_re, left_im = phase_table(outer_size, outer_size, outer_size // 2, -1.0)
    section_re = left_apply(left_re, blocks)
    section_im = left_apply(left_im, blocks)
    twist_re, twist_im = phase_table(period, outer_size, inner_size, -1.0)
    turned_re = section_re * twist_re - section_im * twist_im
    turned_im = section_re * twist_im + section_im * twist_re
    right_re, right_im = phase_table(inner_size, inner_size, inner_size, -1.0)
    spec_re = right_apply(turned_re, right_re) - right_apply(turned_im, right_im)
    spec_im = right_apply(turned_re, right_im) + right_apply(turned_im, right_re)
    return (spec_re, spec_im)


def inverse_signal(spec_re, spec_im, length, inner_size):
    channels_here = spec_re.shape[0]
    period = 2 * length
    outer_size = period // inner_size
    right_re, right_im = phase_table(inner_size, inner_size, inner_size, 1.0)
    mid_re = right_apply(spec_re, right_re) - right_apply(spec_im, right_im)
    mid_im = right_apply(spec_re, right_im) + right_apply(spec_im, right_re)
    twist_re, twist_im = phase_table(period, outer_size, inner_size, 1.0)
    turned_re = mid_re * twist_re - mid_im * twist_im
    turned_im = mid_re * twist_im + mid_im * twist_re
    left_re, left_im = phase_table(outer_size, outer_size // 2, outer_size, 1.0)
    signal = left_apply(left_re, turned_re) - left_apply(left_im, turned_im)
    return signal.reshape(channels_here, length) / period


def long_convolve(signal, filters, inner_size):
    length = signal.shape[1]
    data_re, data_im = forward_spectrum(signal, inner_size)
    filt_re, filt_im = forward_spectrum(filters, inner_size)
    prod_re = data_re * filt_re - data_im * filt_im
    prod_im = data_re * filt_im + data_im * filt_re
    return inverse_signal(prod_re, prod_im, length, inner_size)


def shards(query_proj, key_proj, value_proj, short_taps, long_filters, out_weight):
    tok_rows = query_proj.shape[1]
    inner_size = tok_rows // 2
    tail_cols = jnp.stack([query_proj[:, -2:], key_proj[:, -2:], value_proj[:, -2:]])
    before = shifted(tail_cols, "seq", 1)
    shorts = []
    for stream_index, stream in enumerate((query_proj, key_proj, value_proj)):
        extended = jnp.concatenate([before[stream_index], stream], axis=1).astype(jnp.float32)
        shorts.append(short_filter(extended, short_taps[stream_index]))
    query_short, key_short, value_short = shorts
    product = (key_short * value_short).astype(jnp.bfloat16)
    spread = lax.all_to_all(product, "seq", split_axis=0, concat_axis=1, tiled=True)
    mixed_conv = long_convolve(spread.astype(jnp.float32), long_filters, inner_size)
    returned = lax.all_to_all(mixed_conv, "seq", split_axis=1, concat_axis=0, tiled=True)
    gated_out = (query_short * returned).astype(jnp.bfloat16)
    full_rows = lax.all_gather(gated_out, "tp", axis=0, tiled=True)
    result = lax.dot_general(
        full_rows,
        lax.all_gather(out_weight, "seq", axis=0, tiled=True),
        (((0,), (0,)), ((), ())),
        preferred_element_type=jnp.float32,
    )
    return result.astype(jnp.bfloat16)


def solution(mesh):
    return jax.shard_map(
        shards,
        mesh=mesh,
        in_specs=(
            P("tp", "seq"),
            P("tp", "seq"),
            P("tp", "seq"),
            P(None, None, "tp"),
            P(("tp", "seq"), None),
            P("seq", "tp"),
        ),
        out_specs=P("seq", "tp"),
        check_vma=False,
    )
```

profile of v0, /device:TPU:2, one launch (start us, length us, event | category | flops | bytes accessed | tf_op | source)
XLA Modules:
  0.0 292.9 jit_solution(1270531788461723805)
XLA Ops:
  6.5 1.0 slice.94
  7.6 0.1 copy.35
  7.7 1.0 slice.95
  8.7 0.1 copy.36
  8.8 1.0 slice.96
  9.9 0.1 copy.37
  10.0 0.3 copy.25
  10.3 3.5 %collective-permute-start = (bf16[3,512,2]{2,1,0:T(8,128)(2,1)S(1)}, bf16[3,512,2]{2,1,0:T(8,128)(2,1)S(1)}, u32[]{:S(2)}, u32[]{:S(2)}) collective-permute-start(bf16[3,512,2]{2,1,0:T(8,128)(2,1)S(1)} %copy.25), channel_id=1, source_target_pairs={{0,8},{8,16},{16,24},{24,32},{32,40},{40,48},{48,56},{56,64},{64,7... | collective-permute-start | bytes 18440 | tf_op jit(solution)/shard_map/ppermute | solution.py:13
  13.8 0.3 multiply_sine_fusion.1
  14.1 1.1 reshape.82
  15.2 0.2 copy.29
  15.4 1.1 fusion.58
  16.5 1.1 fusion.61
  17.6 0.9 fusion.180
  18.4 0.8 fusion.4
  19.2 0.8 convolution_add_fusion.1
  20.0 0.3 multiply_sine_fusion
  20.3 1.8 collective-permute-done
  22.2 0.2 maximum_convert_fusion.1
  22.4 1.4 fusion.47
  23.8 20.5 %all-to-all-start = ((bf16[64,8,128]{2,1,0:T(8,128)(2,1)}), bf16[64,8,128]{2,1,0:T(8,128)(2,1)S(1)}, u32[]{:S(2)}, u32[]{:S(2)}) async-start(bf16[64,8,128]{2,1,0:T(8,128)(2,1)} %fusion.47), calls=%async_computation | async-start | bytes 262144 | tf_op jit(solution)/shard_map/all_to_all | solution.py:93
  44.3 0.8 fusion.6
  45.1 0.8 convolution_subtract_fusion.1
  45.9 15.1 %all-to-all-done = bf16[64,8,128]{2,1,0:T(8,128)(2,1)S(1)} async-done(((bf16[64,8,128]{2,1,0:T(8,128)(2,1)}), bf16[64,8,128]{2,1,0:T(8,128)(2,1)S(1)}, u32[]{:S(2)}, u32[]{:S(2)}) %all-to-all-start) | async-done | bytes 131104 | tf_op jit(solution)/shard_map/all_to_all | solution.py:93
  61.0 0.1 reshape.81
  61.1 0.9 convolution_bitcast_fusion
  62.0 0.9 convolution_bitcast_fusion.1
  62.9 0.8 fusion.48
  63.7 0.8 fusion.49
  64.5 0.8 convolution_subtract_fusion.2
  65.3 0.9 multiply_add_fusion
  66.2 0.7 fusion.71
  67.0 0.7 fusion.67
  67.7 0.7 convolution_subtract_fusion
  68.5 0.7 convolution_add_fusion
  69.2 1.1 fusion.11
  70.3 1.1 fusion.1
  71.4 0.2 copy.31
  71.6 0.1 div.13
  71.7 1.1 copy.32
  72.8 4.6 %all-to-all-start.1 = ((f32[8,64,128]{2,0,1:T(8,128)}), f32[8,64,128]{2,0,1:T(8,128)S(1)}, u32[]{:S(2)}, u32[]{:S(2)}) async-start(f32[8,64,128]{2,0,1:T(8,128)} %copy.32), calls=%async_computation.1 | async-start | bytes 524288 | tf_op jit(solution)/shard_map/all_to_all | solution.py:95
  77.5 0.1 maximum_convert_fusion
  77.6 21.1 %all-to-all-done.1 = f32[8,64,128]{2,0,1:T(8,128)S(1)} async-done(((f32[8,64,128]{2,0,1:T(8,128)}), f32[8,64,128]{2,0,1:T(8,128)S(1)}, u32[]{:S(2)}, u32[]{:S(2)}) %all-to-all-start.1) | async-done | bytes 262176 | tf_op jit(solution)/shard_map/all_to_all | solution.py:95
  98.8 1.1 fusion.23
  99.9 0.7 all-gather.5.cloned.1.call-update
  100.6 19.3 %all-gather.3.cloned.1.call-done = bf16[4096,128]{1,0:T(8,128)(2,1)} async-done(((bf16[512,128]{1,0:T(8,128)(2,1)}), bf16[4096,128]{1,0:T(8,128)(2,1)}) %all-gather.3.cloned.1.call-update) | async-done | bytes 1048592 | tf_op jit(solution)/shard_map/all_gather | solution.py:97
  120.0 160.3 %all-gather.5.cloned.1.call-done = bf16[4096,1024]{1,0:T(8,128)(2,1)} async-done(((bf16[64,1024]{1,0:T(8,128)(2,1)}), bf16[4096,1024]{1,0:T(8,128)(2,1)}) %all-gather.5.cloned.1.call-update) | async-done | bytes 8388624 | tf_op jit(solution)/shard_map/all_gather | solution.py:100
  280.3 5.7 %convolution_convert_fusion = bf16[128,1024]{1,0:T(8,128)(2,1)} fusion(bf16[4096,128]{1,0:T(8,128)(2,1)} %all-gather.3.cloned.1.call-done, bf16[4096,1024]{1,0:T(8,128)(2,1)} %all-gather.5.cloned.1.call-done), kind=kOutput, calls=%fused_computation.8 | convolution fusion | flops 1073872896 | bytes 9699328 | tf_op jit(solution)/shard_map/dot_general | solution.py:98
  (12 shorter events, 0.2 us)
Async XLA Ops:
  6.5 15.6 %copy-start.1 = (bf16[512,128]{1,0:T(8,128)(2,1)S(1)}, bf16[512,128]{1,0:T(8,128)(2,1)}, u32[]{:S(2)}) copy-start(bf16[512,128]{1,0:T(8,128)(2,1)} %param.7) | copy-start | bytes 393220
  6.5 15.6 %copy-start = (bf16[512,128]{1,0:T(8,128)(2,1)S(1)}, bf16[512,128]{1,0:T(8,128)(2,1)}, u32[]{:S(2)}) copy-start(bf16[512,128]{1,0:T(8,128)(2,1)} %param.8) | copy-start | bytes 393220
  10.3 11.8 %collective-permute-start = (bf16[3,512,2]{2,1,0:T(8,128)(2,1)S(1)}, bf16[3,512,2]{2,1,0:T(8,128)(2,1)S(1)}, u32[]{:S(2)}, u32[]{:S(2)}) collective-permute-start(bf16[3,512,2]{2,1,0:T(8,128)(2,1)S(1)} %copy.25), channel_id=1, source_target_pairs={{0,8},{8,16},{16,24},{24,32},{32,40},{40,48},{48,56},{56,64},{64,7... | collective-permute-start | bytes 18440 | tf_op jit(solution)/shard_map/ppermute | solution.py:13
  23.8 37.2 %all-to-all-start = ((bf16[64,8,128]{2,1,0:T(8,128)(2,1)}), bf16[64,8,128]{2,1,0:T(8,128)(2,1)S(1)}, u32[]{:S(2)}, u32[]{:S(2)}) async-start(bf16[64,8,128]{2,1,0:T(8,128)(2,1)} %fusion.47), calls=%async_computation | async-start | bytes 262144 | tf_op jit(solution)/shard_map/all_to_all | solution.py:93
  64.5 13.0 %copy-start.2 = (bf16[512,128]{1,0:T(8,128)(2,1)S(1)}, bf16[512,128]{1,0:T(8,128)(2,1)}, u32[]{:S(2)}) copy-start(bf16[512,128]{1,0:T(8,128)(2,1)} %param.6) | copy-start | bytes 393220
  72.8 26.0 %all-to-all-start.1 = ((f32[8,64,128]{2,0,1:T(8,128)}), f32[8,64,128]{2,0,1:T(8,128)S(1)}, u32[]{:S(2)}, u32[]{:S(2)}) async-start(f32[8,64,128]{2,0,1:T(8,128)} %copy.32), calls=%async_computation.1 | async-start | bytes 524288 | tf_op jit(solution)/shard_map/all_to_all | solution.py:95
  77.4 42.5 %all-gather.3.cloned.1.call-start = ((), (), s32[]{:S(2)}) async-start(), calls=%async_computation.2 | async-start | bytes 1179648 | tf_op jit(solution)/shard_map/all_gather | solution.py:97
  99.9 180.4 %all-gather.5.cloned.1.call-start = ((), (), s32[]{:S(2)}) async-start(), calls=%async_computation.3 | async-start | bytes 8519680 | tf_op jit(solution)/shard_map/all_gather | solution.py:100
Sparse Core Ops, SparseCore 0:
  100.0 19.9 all-gather.2
  122.9 157.3 all-gather.4
where the time goes:
time: 293 us
  waiting for transfers between devices  218 us (74%)
  starting transfers between devices  28.7 us (10%)
  matrix products  21.1 us (7%)
  between operations  13.7 us (5%)
  local copies, waits for them, and re-layouts  7.47 us (3%)
  other arithmetic  3.41 us (1%)
    all_gather x1, waiting for transfers between devices, shards(): lax.all_gather(out_weight, 'seq', axis=0, tiled=True)  160 us
    all_to_all x1, waiting for transfers between devices, shards(): lax.all_to_all(mixed_conv, 'seq', split_axis=1, concat_axis=0, tiled=True)  21.1 us
    all_to_all x1, starting transfers between devices, shards(): lax.all_to_all(product, 'seq', split_axis=0, concat_axis=1, tiled=True)  20.5 us
    all_gather x1, waiting for transfers between devices, shards(): full_rows = lax.all_gather(gated_out, 'tp', axis=0, tiled=True)  19.3 us
    all_to_all x1, waiting for transfers between devices, shards(): lax.all_to_all(product, 'seq', split_axis=0, concat_axis=1, tiled=True)  15.1 us
    dot_general x12, matrix products, right_apply(): return jnp.einsum('ckn,nm->ckm', signal, phase, precision=precise)  9.29 us
  transfers between devices with their start and end apart: 5, of which 5 were waited for; matrix products, arithmetic and copies ran while one was open for 3% of the time, Pallas kernels for 0%

commit v1 on v0

--- a/solution.py
+++ b/solution.py
@@ -5,6 +5,19 @@
 from jax.sharding import PartitionSpec as P
 
 precise = lax.Precision.HIGHEST
+
+
+def collect(x, axis, dim):
+    ways = lax.axis_size(axis)
+    up = [(d, (d + 1) % ways) for d in range(ways)]
+    down = [(d, (d - 1) % ways) for d in range(ways)]
+    earlier, later = ([x], [x])
+    for _ in range(ways // 2):
+        earlier.append(lax.ppermute(earlier[-1], axis, up))
+    for _ in range((ways - 1) // 2):
+        later.append(lax.ppermute(later[-1], axis, down))
+    line = jnp.concatenate([*earlier[::-1], *later[1:]], axis=dim)
+    return jnp.roll(line, (lax.axis_index(axis) - ways // 2) * x.shape[dim], axis=dim)
 
 
 def shifted(value, axis, steps):
@@ -94,7 +107,7 @@
     mixed_conv = long_convolve(spread.astype(jnp.float32), long_filters, inner_size)
     returned = lax.all_to_all(mixed_conv, "seq", split_axis=1, concat_axis=0, tiled=True)
     gated_out = (query_short * returned).astype(jnp.bfloat16)
-    full_rows = lax.all_gather(gated_out, "tp", axis=0, tiled=True)
+    full_rows = collect(gated_out, "tp", 0)
     result = lax.dot_general(
         full_rows,
         lax.all_gather(out_weight, "seq", axis=0, tiled=True),

time: 293 us -> 186 us (0.63)
  waiting for transfers between devices: 218 us -> 107 us
  starting transfers between devices: 28.7 us -> 34.9 us
    all_gather x1, waiting for transfers between devices: 160 us -> 53.6 us  [shards(): lax.all_gather(out_weight, 'seq', axis=0, tiled=True)]
    all_gather x1 -> x0, waiting for transfers between devices: 19.3 us -> none  [shards(): full_rows = lax.all_gather(gated_out, 'tp', axis=0, tiled=True)]
    ppermute x0 -> x7, waiting for transfers between devices: none -> 11.9 us  [the longest x4 11.1 us: collect(): earlier.append(lax.ppermute(earlier[-1], axis, up))]
    ppermute x0 -> x7, starting transfers between devices: none -> 6.18 us  [the longest x3 6.15 us: collect(): later.append(lax.ppermute(later[-1], axis, down))]
  transfers between devices with their start and end apart: 5 -> 11, of which waited for: 5 -> 10; matrix products, arithmetic and copies ran while one was open for 3% -> 13% of each run, Pallas kernels for 0% -> 0%
where the time goes in v1:
time: 186 us
  waiting for transfers between devices  107 us (58%)
  starting transfers between devices  34.9 us (19%)
  matrix products  20.8 us (11%)
  between operations  13.8 us (7%)
  local copies, waits for them, and re-layouts  6.88 us (4%)
  other arithmetic  2.75 us (1%)
    all_gather x1, waiting for transfers between devices, shards(): lax.all_gather(out_weight, 'seq', axis=0, tiled=True)  53.6 us
    all_to_all x1, waiting for transfers between devices, shards(): lax.all_to_all(mixed_conv, 'seq', split_axis=1, concat_axis=0, tiled=True)  21.9 us
    all_to_all x1, starting transfers between devices, shards(): lax.all_to_all(product, 'seq', split_axis=0, concat_axis=1, tiled=True)  20.5 us
    all_to_all x1, waiting for transfers between devices, shards(): lax.all_to_all(product, 'seq', split_axis=0, concat_axis=1, tiled=True)  16 us
    ppermute x4, waiting for transfers between devices, collect(): earlier.append(lax.ppermute(earlier[-1], axis, up))  11.1 us
    dot_general x12, matrix products, right_apply(): return jnp.einsum('ckn,nm->ckm', signal, phase, precision=precise)  9.31 us
    ppermute x3, starting transfers between devices, collect(): later.append(lax.ppermute(later[-1], axis, down))  6.15 us
    dot_general x1, matrix products, shards(): lax.dot_general(full_rows, lax.all_gather(out_weight, 'seq', axis=0, tile...  5.37 us
  transfers between devices with their start and end apart: 11, of which 10 were waited for; matrix products, arithmetic and copies ran while one was open for 13% of the time, Pallas kernels for 0%

profile of v1, /device:TPU:2, one launch (start us, length us, event | category | flops | bytes accessed | tf_op | source)
XLA Modules:
  0.0 185.9 jit_solution(11645864898718294468)
XLA Ops:
  6.5 0.7 all-gather.2.cloned.1.call-update
  7.3 1.0 slice.94
  8.4 1.0 slice.95
  9.5 1.0 slice.96
  10.7 0.3 copy.25
  10.9 3.5 %collective-permute-start = (bf16[3,512,2]{2,1,0:T(8,128)(2,1)S(1)}, bf16[3,512,2]{2,1,0:T(8,128)(2,1)S(1)}, u32[]{:S(2)}, u32[]{:S(2)}) collective-permute-start(bf16[3,512,2]{2,1,0:T(8,128)(2,1)S(1)} %copy.25), channel_id=1, source_target_pairs={{0,8},{8,16},{16,24},{24,32},{32,40},{40,48},{48,56},{56,64},{64,7... | collective-permute-start | bytes 18440 | tf_op jit(solution)/shard_map/ppermute | solution.py:26
  14.5 1.1 reshape.82
  15.8 0.3 multiply_sine_fusion.1
  16.1 1.1 fusion.59
  17.2 1.1 fusion.62
  18.3 0.8 fusion.5
  19.1 0.8 convolution_add_fusion.1
  19.9 0.3 multiply_sine_fusion
  20.1 2.6 %collective-permute-done = bf16[3,512,2]{2,1,0:T(8,128)(2,1)S(1)} collective-permute-done((bf16[3,512,2]{2,1,0:T(8,128)(2,1)S(1)}, bf16[3,512,2]{2,1,0:T(8,128)(2,1)S(1)}, u32[]{:S(2)}, u32[]{:S(2)}) %collective-permute-start) | collective-permute-done | bytes 6176 | tf_op jit(solution)/shard_map/ppermute | solution.py:26
  22.8 0.2 maximum_convert_fusion.1
  23.1 1.4 fusion.48
  24.5 20.5 %all-to-all-start = ((bf16[64,8,128]{2,1,0:T(8,128)(2,1)}), bf16[64,8,128]{2,1,0:T(8,128)(2,1)S(1)}, u32[]{:S(2)}, u32[]{:S(2)}) async-start(bf16[64,8,128]{2,1,0:T(8,128)(2,1)} %fusion.48), calls=%async_computation | async-start | bytes 262144 | tf_op jit(solution)/shard_map/all_to_all | solution.py:106
  45.0 0.8 fusion.7
  45.8 0.8 convolution_subtract_fusion.1
  46.6 16.0 %all-to-all-done = bf16[64,8,128]{2,1,0:T(8,128)(2,1)S(1)} async-done(((bf16[64,8,128]{2,1,0:T(8,128)(2,1)}), bf16[64,8,128]{2,1,0:T(8,128)(2,1)S(1)}, u32[]{:S(2)}, u32[]{:S(2)}) %all-to-all-start) | async-done | bytes 131104 | tf_op jit(solution)/shard_map/all_to_all | solution.py:106
  62.7 0.9 convolution_bitcast_fusion
  63.6 0.9 convolution_bitcast_fusion.1
  64.5 0.8 fusion.50
  65.3 0.8 fusion.49
  66.1 0.8 convolution_subtract_fusion.2
  66.9 0.9 multiply_add_fusion
  67.8 0.7 fusion.72
  68.6 0.7 fusion.68
  69.3 0.7 convolution_subtract_fusion
  70.0 0.7 convolution_add_fusion
  70.8 1.1 fusion.12
  71.9 1.1 fusion.1
  73.0 0.2 copy.31
  73.3 1.1 copy.32
  74.4 4.7 %all-to-all-start.1 = ((f32[8,64,128]{2,0,1:T(8,128)}), f32[8,64,128]{2,0,1:T(8,128)S(1)}, u32[]{:S(2)}, u32[]{:S(2)}) async-start(f32[8,64,128]{2,0,1:T(8,128)} %copy.32), calls=%async_computation.1 | async-start | bytes 524288 | tf_op jit(solution)/shard_map/all_to_all | solution.py:108
  79.3 21.9 %all-to-all-done.1 = f32[8,64,128]{2,0,1:T(8,128)S(1)} async-done(((f32[8,64,128]{2,0,1:T(8,128)}), f32[8,64,128]{2,0,1:T(8,128)S(1)}, u32[]{:S(2)}, u32[]{:S(2)}) %all-to-all-start.1) | async-done | bytes 262176 | tf_op jit(solution)/shard_map/all_to_all | solution.py:108
  101.2 0.4 fusion.24
  101.6 4.4 %collective-permute-done.1 = bf16[512,128]{1,0:T(8,128)(2,1)S(1)} collective-permute-done((bf16[512,128]{1,0:T(8,128)(2,1)S(1)}, bf16[512,128]{1,0:T(8,128)(2,1)S(1)}, u32[]{:S(2)}, u32[]{:S(2)}) %collective-permute-start.1) | collective-permute-done | bytes 131104 | tf_op jit(solution)/shard_map/ppermute | solution.py:16
  106.0 1.7 collective-permute-start.5
  107.7 2.6 %collective-permute-done.2 = bf16[512,128]{1,0:T(8,128)(2,1)S(1)} collective-permute-done((bf16[512,128]{1,0:T(8,128)(2,1)S(1)}, bf16[512,128]{1,0:T(8,128)(2,1)S(1)}, u32[]{:S(2)}, u32[]{:S(2)}) %collective-permute-start.2) | collective-permute-done | bytes 131104 | tf_op jit(solution)/shard_map/ppermute | solution.py:16
  110.4 2.1 %collective-permute-start.6 = (bf16[512,128]{1,0:T(8,128)(2,1)S(1)}, bf16[512,128]{1,0:T(8,128)(2,1)S(1)}, u32[]{:S(2)}, u32[]{:S(2)}) collective-permute-start(bf16[512,128]{1,0:T(8,128)(2,1)S(1)} %collective-permute-done.5), channel_id=1, source_target_pairs={{0,7},{1,0},{2,1},{3,2},{4,3},{5,4},{6,5},{7,6},{8,15},{9,8},{10,9... | collective-permute-start | bytes 393224 | tf_op jit(solution)/shard_map/ppermute | solution.py:18
  112.5 2.2 %collective-permute-done.3 = bf16[512,128]{1,0:T(8,128)(2,1)S(1)} collective-permute-done((bf16[512,128]{1,0:T(8,128)(2,1)S(1)}, bf16[512,128]{1,0:T(8,128)(2,1)S(1)}, u32[]{:S(2)}, u32[]{:S(2)}) %collective-permute-start.3) | collective-permute-done | bytes 131104 | tf_op jit(solution)/shard_map/ppermute | solution.py:16
  114.8 0.3 collective-permute-done.6
  115.0 2.3 %collective-permute-start.7 = (bf16[512,128]{1,0:T(8,128)(2,1)S(1)}, bf16[512,128]{1,0:T(8,128)(2,1)S(1)}, u32[]{:S(2)}, u32[]{:S(2)}) collective-permute-start(bf16[512,128]{1,0:T(8,128)(2,1)S(1)} %collective-permute-done.6), channel_id=1, source_target_pairs={{0,7},{1,0},{2,1},{3,2},{4,3},{5,4},{6,5},{7,6},{8,15},{9,8},{10,9... | collective-permute-start | bytes 393224 | tf_op jit(solution)/shard_map/ppermute | solution.py:18
  117.3 1.8 collective-permute-done.4
  119.3 0.5 collective-permute-done.7
  120.1 53.6 %all-gather.2.cloned.1.call-done = bf16[4096,1024]{1,0:T(8,128)(2,1)} async-done(((bf16[64,1024]{1,0:T(8,128)(2,1)}), bf16[4096,1024]{1,0:T(8,128)(2,1)}) %all-gather.2.cloned.1.call-update) | async-done | bytes 8388624 | tf_op jit(solution)/shard_map/all_gather | solution.py:113
  173.7 5.4 %convolution_convert_fusion = bf16[128,1024]{1,0:T(8,128)(2,1)} fusion(bf16[4096,1024]{1,0:T(8,128)(2,1)} %all-gather.2.cloned.1.call-done, bf16[8192,128]{1,0:T(8,128)(2,1)S(1)} %constant_dynamic-update-slice_fusion, s32[]{:T(128)S(6)} %select_n.117), kind=kOutput, calls=%fused_computation.8 | convolution fusion | flops 1073872896 | bytes 9699332 | tf_op jit(solution)/shard_map/dot_general | solution.py:111
  (41 shorter events, 1.4 us)
Async XLA Ops:
  6.5 9.5 %copy-start.3 = (f32[3,3,512]{2,1,0:T(4,128)S(1)}, f32[3,3,512]{2,1,0:T(4,128)}, u32[]{:S(2)}) copy-start(f32[3,3,512]{2,1,0:T(4,128)} %param.9) | copy-start | bytes 55300
  6.5 167.1 %all-gather.2.cloned.1.call-start = ((), (), s32[]{:S(2)}) async-start(), calls=%async_computation.2 | async-start | bytes 8519680 | tf_op jit(solution)/shard_map/all_gather | solution.py:113
  10.9 11.8 %collective-permute-start = (bf16[3,512,2]{2,1,0:T(8,128)(2,1)S(1)}, bf16[3,512,2]{2,1,0:T(8,128)(2,1)S(1)}, u32[]{:S(2)}, u32[]{:S(2)}) collective-permute-start(bf16[3,512,2]{2,1,0:T(8,128)(2,1)S(1)} %copy.25), channel_id=1, source_target_pairs={{0,8},{8,16},{16,24},{24,32},{32,40},{40,48},{48,56},{56,64},{64,7... | collective-permute-start | bytes 18440 | tf_op jit(solution)/shard_map/ppermute | solution.py:26
  18.3 4.5 %copy-start = (bf16[512,128]{1,0:T(8,128)(2,1)S(1)}, bf16[512,128]{1,0:T(8,128)(2,1)}, u32[]{:S(2)}) copy-start(bf16[512,128]{1,0:T(8,128)(2,1)} %param.8) | copy-start | bytes 393220
  18.3 4.5 %copy-start.1 = (bf16[512,128]{1,0:T(8,128)(2,1)S(1)}, bf16[512,128]{1,0:T(8,128)(2,1)}, u32[]{:S(2)}) copy-start(bf16[512,128]{1,0:T(8,128)(2,1)} %param.7) | copy-start | bytes 393220
  24.5 38.1 %all-to-all-start = ((bf16[64,8,128]{2,1,0:T(8,128)(2,1)}), bf16[64,8,128]{2,1,0:T(8,128)(2,1)S(1)}, u32[]{:S(2)}, u32[]{:S(2)}) async-start(bf16[64,8,128]{2,1,0:T(8,128)(2,1)} %fusion.48), calls=%async_computation | async-start | bytes 262144 | tf_op jit(solution)/shard_map/all_to_all | solution.py:106
  71.9 7.2 %copy-start.2 = (bf16[512,128]{1,0:T(8,128)(2,1)S(1)}, bf16[512,128]{1,0:T(8,128)(2,1)}, u32[]{:S(2)}) copy-start(bf16[512,128]{1,0:T(8,128)(2,1)} %param.6) | copy-start | bytes 393220
  74.4 26.7 %all-to-all-start.1 = ((f32[8,64,128]{2,0,1:T(8,128)}), f32[8,64,128]{2,0,1:T(8,128)S(1)}, u32[]{:S(2)}, u32[]{:S(2)}) async-start(f32[8,64,128]{2,0,1:T(8,128)} %copy.32), calls=%async_computation.1 | async-start | bytes 524288 | tf_op jit(solution)/shard_map/all_to_all | solution.py:108
  101.6 4.4 %collective-permute-start.1 = (bf16[512,128]{1,0:T(8,128)(2,1)S(1)}, bf16[512,128]{1,0:T(8,128)(2,1)S(1)}, u32[]{:S(2)}, u32[]{:S(2)}) collective-permute-start(bf16[512,128]{1,0:T(8,128)(2,1)S(1)} %fusion.24), channel_id=1, source_target_pairs={{0,1},{1,2},{2,3},{3,4},{4,5},{5,6},{6,7},{7,0},{8,9},{9,10},{10,1... | collective-permute-start | bytes 393224 | tf_op jit(solution)/shard_map/ppermute | solution.py:16
  106.0 4.4 %collective-permute-start.2 = (bf16[512,128]{1,0:T(8,128)(2,1)S(1)}, bf16[512,128]{1,0:T(8,128)(2,1)S(1)}, u32[]{:S(2)}, u32[]{:S(2)}) collective-permute-start(bf16[512,128]{1,0:T(8,128)(2,1)S(1)} %collective-permute-done.1), channel_id=1, source_target_pairs={{0,1},{1,2},{2,3},{3,4},{4,5},{5,6},{6,7},{7,0},{8,9},{9,10},{10,1... | collective-permute-start | bytes 393224 | tf_op jit(solution)/shard_map/ppermute | solution.py:16
  106.0 4.4 %collective-permute-start.5 = (bf16[512,128]{1,0:T(8,128)(2,1)S(1)}, bf16[512,128]{1,0:T(8,128)(2,1)S(1)}, u32[]{:S(2)}, u32[]{:S(2)}) collective-permute-start(bf16[512,128]{1,0:T(8,128)(2,1)S(1)} %fusion.24), channel_id=1, source_target_pairs={{0,7},{1,0},{2,1},{3,2},{4,3},{5,4},{6,5},{7,6},{8,15},{9,8},{10,9... | collective-permute-start | bytes 393224 | tf_op jit(solution)/shard_map/ppermute | solution.py:18
  110.4 4.4 %collective-permute-start.3 = (bf16[512,128]{1,0:T(8,128)(2,1)S(1)}, bf16[512,128]{1,0:T(8,128)(2,1)S(1)}, u32[]{:S(2)}, u32[]{:S(2)}) collective-permute-start(bf16[512,128]{1,0:T(8,128)(2,1)S(1)} %collective-permute-done.2), channel_id=1, source_target_pairs={{0,1},{1,2},{2,3},{3,4},{4,5},{5,6},{6,7},{7,0},{8,9},{9,10},{10,1... | collective-permute-start | bytes 393224 | tf_op jit(solution)/shard_map/ppermute | solution.py:16
  110.4 4.7 %collective-permute-start.6 = (bf16[512,128]{1,0:T(8,128)(2,1)S(1)}, bf16[512,128]{1,0:T(8,128)(2,1)S(1)}, u32[]{:S(2)}, u32[]{:S(2)}) collective-permute-start(bf16[512,128]{1,0:T(8,128)(2,1)S(1)} %collective-permute-done.5), channel_id=1, source_target_pairs={{0,7},{1,0},{2,1},{3,2},{4,3},{5,4},{6,5},{7,6},{8,15},{9,8},{10,9... | collective-permute-start | bytes 393224 | tf_op jit(solution)/shard_map/ppermute | solution.py:18
  114.8 4.4 %collective-permute-start.4 = (bf16[512,128]{1,0:T(8,128)(2,1)S(1)}, bf16[512,128]{1,0:T(8,128)(2,1)S(1)}, u32[]{:S(2)}, u32[]{:S(2)}) collective-permute-start(bf16[512,128]{1,0:T(8,128)(2,1)S(1)} %collective-permute-done.3), channel_id=1, source_target_pairs={{0,1},{1,2},{2,3},{3,4},{4,5},{5,6},{6,7},{7,0},{8,9},{9,10},{10,1... | collective-permute-start | bytes 393224 | tf_op jit(solution)/shard_map/ppermute | solution.py:16
  115.0 4.8 %collective-permute-start.7 = (bf16[512,128]{1,0:T(8,128)(2,1)S(1)}, bf16[512,128]{1,0:T(8,128)(2,1)S(1)}, u32[]{:S(2)}, u32[]{:S(2)}) collective-permute-start(bf16[512,128]{1,0:T(8,128)(2,1)S(1)} %collective-permute-done.6), channel_id=1, source_target_pairs={{0,7},{1,0},{2,1},{3,2},{4,3},{5,4},{6,5},{7,6},{8,15},{9,8},{10,9... | collective-permute-start | bytes 393224 | tf_op jit(solution)/shard_map/ppermute | solution.py:18
Sparse Core Ops, SparseCore 0:
  10.3 163.3 all-gather.1
